TPU v7x, 32 devices: a whole 2x2x4 slice. The times are simulated.
32 devices in a mesh: section: 4 (over y, x), student: 2 (over core), dp: 4 (over z).
Axes of the slice: x: 2, y: 2, z: 4, core: 2. Of those that a mesh axis runs over, the one named last changes fastest.
Arguments:
- in_flight: bfloat16 [4, 2, 128, 4096], P('section', 'student'), may hold values from -6 to 6
- segments: int32 [4, 2, 128], P(None, 'student'), may hold values from 0 to 3, never falling along the last dimension, each value on 1 to 64 neighbouring positions
- norm_gain: float32 [4, 4096], P('section'), may hold values from 0.5 to 1.5
- w_qkv: bfloat16 [4, 4096, 3, 1024], P('section', None, None, 'dp')
- w_out: bfloat16 [4, 1024, 4096], P('section', 'dp'), may hold values from -0.1875 to 0.1875
- final_gain: float32 [4096], replicated, may hold values from 0.25 to 1.75
- student_rows: bfloat16 [2, 3, 2, 128, 1024], P('student', None, None, 'dp'), may hold values from -6 to 6
- student_gain: float32 [2, 1024], P('student'), may hold values from 0.5 to 1.5
- w_head: bfloat16 [2, 1024, 4096], P('student', None, 'section'), may hold values from -0.1875 to 0.1875
Outputs:
- advanced: bfloat16 [4, 2, 128, 4096], P('section', 'student', 'dp')
- grad_head: float32 [2, 1024, 4096], P('student', 'dp', 'section')
Inputs may be any that keep to these rules, and one draw needn't show every extreme that they name: `segments`: along a micro-batch's tokens the crop numbers never fall; each of the 4 crops holds 1 to 64 tokens and one holds exactly 64.
All inputs are finite; a program needn't handle non-finite values.
Results may differ from a plain program's by a relative error of at most 0.025.
Values may be sent and summed in bfloat16 or wider, within the bound.
A program may use at most 64 MiB of HBM per device.

v0:
```python
import jax
import jax.numpy as jnp
from jax import lax
from jax.sharding import PartitionSpec as P

HEAD_SIZE = 128
TOK = 128


def shifted(x, axis, by):
    count = lax.axis_size(axis)
    pairs = [(i, i + by) for i in range(count) if 0 <= i + by < count]
    return lax.ppermute(x, axis, pairs)


def broadcast(value, axis, source):
    kept = jnp.where(lax.axis_index(axis) == source, value, 0).astype(value.dtype)
    return lax.psum(kept, axis)


def layer_norm(rows, gain):
    rows = rows.astype(jnp.float32)
    centred = rows - jnp.mean(rows, axis=-1, keepdims=True)
    spread = jnp.mean(centred * centred, axis=-1, keepdims=True)
    return centred * lax.rsqrt(spread + 1e-06) * gain


def attend(state, crops, gain, weights_qkv, weights_out):
    tokens = state.shape[0]
    width = weights_out.shape[0]
    heads = width // HEAD_SIZE
    normed = layer_norm(state, gain).astype(jnp.bfloat16)
    qkv = jnp.dot(normed, weights_qkv, preferred_element_type=jnp.float32).astype(jnp.bfloat16)
    query = qkv[:, :width].reshape(tokens, heads, HEAD_SIZE)
    keys = qkv[:, width : 2 * width].reshape(tokens, heads, HEAD_SIZE)
    values = qkv[:, 2 * width :].reshape(tokens, heads, HEAD_SIZE)
    scores = jnp.einsum(
        "qhd,khd->hqk", query, keys, preferred_element_type=jnp.float32
    ) * HEAD_SIZE ** (-0.5)
    same = crops[:, None] == crops[None, :]
    scores = jnp.where(same[None], scores, -1e30)
    top = jnp.max(scores, axis=-1, keepdims=True)
    expo = jnp.exp(scores - top)
    probs = (expo / jnp.sum(expo, axis=-1, keepdims=True)).astype(jnp.bfloat16)
    mixed = jnp.einsum("hqk,khd->qhd", probs, values, preferred_element_type=jnp.float32).astype(
        jnp.bfloat16
    )
    return jnp.dot(mixed.reshape(tokens, width), weights_out, preferred_element_type=jnp.float32)


def on_device(
    in_flight, segments, norm_gain, w_qkv, w_out, final_gain, student_rows, student_gain, w_head
):
    section = lax.axis_index("section")
    root = lax.axis_size("section") - 1
    share = in_flight.shape[2] // lax.axis_size("dp")
    first_row = lax.axis_index("dp") * share
    ticks = student_rows.shape[1]
    model_width = in_flight.shape[3]
    weights_qkv = w_qkv[0].reshape(model_width, -1)
    weights_out = w_out[0]
    gain = norm_gain[0]
    crop_table = segments[:, 0, :]
    finals = []
    whole = in_flight[0, 0]
    own_rows = lax.dynamic_slice_in_dim(whole, first_row, share, 0)
    for tick in range(ticks):
        if tick > 0:
            whole = lax.all_gather(own_rows, "dp", axis=0, tiled=True)
        crops = lax.dynamic_index_in_dim(crop_table, section - tick, 0, keepdims=False)
        partial_value = attend(whole, crops, gain, weights_qkv, weights_out)
        summed = lax.psum_scatter(
            partial_value.astype(jnp.bfloat16), "dp", scatter_dimension=0, tiled=True
        ).astype(jnp.float32)
        own_rows = (own_rows.astype(jnp.float32) + summed).astype(jnp.bfloat16)
        finals.append(layer_norm(own_rows, final_gain).astype(jnp.bfloat16))
        own_rows = shifted(own_rows, "section", 1)
    advanced = own_rows[None, None]
    finished = jnp.stack(finals)[:, None]
    block = w_head.shape[2]
    block_start = section * block
    columns = lax.all_gather(finished, "student", axis=1, tiled=True)
    spread_rows = broadcast(columns, "section", root)
    targets = lax.dynamic_slice_in_dim(spread_rows, block_start, block, 3)
    student_width = student_rows.shape[4]
    feats = (
        layer_norm(student_rows[0], student_gain[0]).astype(jnp.bfloat16).reshape(-1, student_width)
    )
    pred = jnp.dot(feats, w_head[0], preferred_element_type=jnp.float32)
    err = ((pred - targets.reshape(-1, block).astype(jnp.float32)) * (2.0 / TOK)).astype(
        jnp.bfloat16
    )
    term = lax.dot_general(feats, err, (((0,), (0,)), ((), ())), preferred_element_type=jnp.float32)
    grad = lax.psum_scatter(
        term.astype(jnp.bfloat16), "dp", scatter_dimension=0, tiled=True
    ).astype(jnp.float32)
    return (advanced, grad[None])


def solution(mesh):
    in_specs = (
        P("section", "student", None, None),
        P(None, "student", None),
        P("section", None),
        P("section", None, None, "dp"),
        P("section", "dp", None),
        P(),
        P("student", None, None, "dp", None),
        P("student", None),
        P("student", None, "section"),
    )
    out_specs = (P("section", "student", "dp", None), P("student", "dp", "section"))
    return jax.shard_map(
        on_device, mesh=mesh, in_specs=in_specs, out_specs=out_specs, check_vma=False
    )
```

profile of v0, /device:TPU:0, one launch (start us, length us, event | category | flops | bytes accessed | tf_op | source)
XLA Modules:
  0.0 340.8 jit_solution(15224556704318031938)
XLA Ops:
  7.2 0.8 fusion.103
  8.1 0.1 broadcast_compare_fusion.2
  8.2 8.9 %copy.23 = bf16[1,4096,3,256]{1,3,2,0:T(8,128)(2,1)} copy(bf16[1,4096,3,256]{3,1,2,0:T(8,128)(2,1)} %param.12) | data formatting | bytes 12582912 | tf_op args[3]
  17.1 0.2 convert_reduce_fusion
  17.3 0.4 fusion.18
  17.8 5.0 %convolution_convert_fusion.6 = bf16[128,768]{1,0:T(8,128)(2,1)S(1)} fusion(bf16[4096,768]{0,1:T(8,128)(2,1)} %bitcast.129, bf16[1,1,128,4096]{3,2,1,0:T(8,128)(2,1)S(1)} %copy-done.2, f32[4096]{0:T(1024)S(1)} %bitcast.144, f32[128]{0:T(128)S(1)} %add_rsqrt_fusion.6, f32[128]{0:T(128)S(1)} %broadcast_multiply_fusion.6), kind=kOutput, calls=%fused_computation.41 | convolution fusion | flops 808026112 | bytes 7554048 | tf_op jit(solution)/shard_map/dot_general | solution.py:33
  22.8 0.2 fusion.41
  23.0 0.1 fusion.106
  23.1 0.1 copy.39
  23.2 0.2 convolution_convert_fusion.9
  23.4 1.4 convolution_convert_fusion.2
  24.9 30.1 %reduce-scatter.5.cloned.1.call-done = bf16[32,4096]{1,0:T(8,128)(2,1)} async-done(((bf16[128,4096]{1,0:T(8,128)(2,1)}), bf16[32,4096]{1,0:T(8,128)(2,1)}) %reduce-scatter.5.cloned.1.call-update) | async-done | bytes 262160 | tf_op jit(solution)/shard_map/reduce_scatter | solution.py:72
  55.0 1.1 convert_reduce_fusion.5
  56.1 3.4 collective-permute-start
  59.5 5.1 %collective-permute-done = bf16[32,4096]{1,0:T(8,128)(2,1)S(1)} collective-permute-done((bf16[32,4096]{1,0:T(8,128)(2,1)S(1)}, bf16[32,4096]{1,0:T(8,128)(2,1)S(1)}, u32[]{:S(2)}, u32[]{:S(2)}) %collective-permute-start) | collective-permute-done | bytes 262176 | tf_op jit(solution)/shard_map/ppermute | solution.py:13
  64.7 0.7 copy-done.7
  65.4 0.0 reduce-scatter.7.cloned.1.call-start
  65.5 0.1 broadcast_compare_fusion
  65.6 27.8 %all-gather.5.cloned.1.call-done = bf16[128,4096]{1,0:T(8,128)(2,1)} async-done(((bf16[32,4096]{1,0:T(8,128)(2,1)}), bf16[128,4096]{1,0:T(8,128)(2,1)}) %all-gather.5.cloned.1.call-update) | async-done | bytes 1048592 | tf_op jit(solution)/shard_map/all_gather | solution.py:69
  93.4 1.5 convert_reduce_fusion.2
  95.0 1.7 fusion.10
  96.6 5.0 %convolution_convert_fusion.5 = bf16[128,768]{1,0:T(8,128)(2,1)S(1)} fusion(bf16[4096,768]{0,1:T(8,128)(2,1)} %bitcast.130, bf16[128,4096]{1,0:T(8,128)(2,1)S(1)} %copy-done.3, f32[4096]{0:T(1024)S(1)} %bitcast.145, f32[128]{0:T(128)S(1)} %add_rsqrt_fusion.5, f32[128]{0:T(128)S(1)} %broadcast_multiply_fusion.5), kind=kOutput, calls=%fused_computation.40 | convolution fusion | flops 808026112 | bytes 7554048 | tf_op jit(solution)/shard_map/dot_general | solution.py:33
  101.7 0.2 fusion.42
  101.9 0.1 fusion.107
  101.9 0.1 copy.40
  102.0 0.2 convolution_convert_fusion.8
  102.2 1.4 convolution_convert_fusion.1
  103.8 26.8 %reduce-scatter.7.cloned.1.call-done = bf16[32,4096]{1,0:T(8,128)(2,1)} async-done(((bf16[128,4096]{1,0:T(8,128)(2,1)}), bf16[32,4096]{1,0:T(8,128)(2,1)}) %reduce-scatter.7.cloned.1.call-update) | async-done | bytes 262160 | tf_op jit(solution)/shard_map/reduce_scatter | solution.py:72
  130.5 1.1 convert_reduce_fusion.4
  131.7 3.4 collective-permute-start.1
  135.1 5.1 %collective-permute-done.1 = bf16[32,4096]{1,0:T(8,128)(2,1)S(1)} collective-permute-done((bf16[32,4096]{1,0:T(8,128)(2,1)S(1)}, bf16[32,4096]{1,0:T(8,128)(2,1)S(1)}, u32[]{:S(2)}, u32[]{:S(2)}) %collective-permute-start.1) | collective-permute-done | bytes 262176 | tf_op jit(solution)/shard_map/ppermute | solution.py:13
  140.2 0.7 copy-done.5
  141.0 27.9 %all-gather.7.cloned.1.call-done = bf16[128,4096]{1,0:T(8,128)(2,1)} async-done(((bf16[32,4096]{1,0:T(8,128)(2,1)}), bf16[128,4096]{1,0:T(8,128)(2,1)}) %all-gather.7.cloned.1.call-update) | async-done | bytes 1048592 | tf_op jit(solution)/shard_map/all_gather | solution.py:69
  168.9 1.5 convert_reduce_fusion.1
  170.5 1.7 fusion.7
  172.1 5.0 %convolution_convert_fusion.4 = bf16[128,768]{1,0:T(8,128)(2,1)S(1)} fusion(bf16[4096,768]{0,1:T(8,128)(2,1)} %bitcast.131, bf16[128,4096]{1,0:T(8,128)(2,1)S(1)} %copy-done.4, f32[128]{0:T(128)S(1)} %add_rsqrt_fusion.4, f32[128]{0:T(128)S(1)} %broadcast_multiply_fusion.4, f32[4096]{0:T(1024)S(1)} %bitcast.146), kind=kOutput, calls=%fused_computation.39 | convolution fusion | flops 808026112 | bytes 7554048 | tf_op jit(solution)/shard_map/dot_general | solution.py:33
  177.2 0.2 fusion.43
  177.4 0.1 fusion.108
  177.4 0.1 copy.41
  177.5 0.2 convolution_convert_fusion.7
  177.7 1.4 convolution_convert_fusion
  179.3 0.3 fusion.75
  179.6 0.3 fusion.72
  179.8 26.2 %reduce-scatter.9.cloned.1.call-done = bf16[32,4096]{1,0:T(8,128)(2,1)} async-done(((bf16[128,4096]{1,0:T(8,128)(2,1)}), bf16[32,4096]{1,0:T(8,128)(2,1)}) %reduce-scatter.9.cloned.1.call-update) | async-done | bytes 262160 | tf_op jit(solution)/shard_map/reduce_scatter | solution.py:72
  206.0 1.1 convert_reduce_fusion.3
  207.2 0.3 fusion.69
  207.5 0.3 fusion.80
  207.8 1.0 pad_maximum_fusion
  208.8 8.4 %all-gather.9.cloned.1.call-done = bf16[3,64,4096]{2,1,0:T(8,128)(2,1)} async-done(((bf16[3,32,4096]{2,1,0:T(8,128)(2,1)}), bf16[3,64,4096]{2,1,0:T(8,128)(2,1)}) %all-gather.9.cloned.1.call-update) | async-done | bytes 1572880 | tf_op jit(solution)/shard_map/all_gather | solution.py:82
  217.2 1.3 broadcast_select_fusion
  218.6 0.1 convert_reduce_fusion.6
  218.7 0.1 div.81
  218.8 0.2 fusion.59
  219.0 0.1 rsqrt.64
  219.1 0.3 fusion.62
  219.4 0.2 multiply_convert_fusion
  219.7 62.6 %all-reduce.2.cloned.1.call-done = bf16[3,2,32,4096]{3,2,1,0:T(8,128)(2,1)} async-done(((bf16[3,2,32,4096]{3,2,1,0:T(8,128)(2,1)}), bf16[3,2,32,4096]{3,2,1,0:T(8,128)(2,1)}) %all-reduce.2.cloned.1.call-update) | async-done | bytes 1572880 | tf_op jit(solution)/shard_map/psum | solution.py:18
  282.3 1.0 constant_dynamic-slice_fusion
  283.3 4.1 %convolution_convert_fusion.3 = bf16[1024,1024]{1,0:T(8,128)(2,1)} fusion(bf16[192,1024]{1,0:T(8,128)(2,1)S(1)} %fusion.62, bf16[192,1024]{1,0:T(8,128)(2,1)S(1)} %bitcast.133, bf16[1,1024,1024]{2,1,0:T(8,128)(2,1)} %param.17, bf16[192,1024]{1,0:T(8,128)(2,1)S(1)} %bitcast.134), kind=kOutput, calls=%fused_computation.34 | convolution fusion | flops 807141376 | bytes 5373952 | tf_op jit(solution)/shard_map/dot_general | solution.py:93
  287.4 3.4 collective-permute-start.2
  290.8 5.4 %collective-permute-done.2 = bf16[32,4096]{1,0:T(8,128)(2,1)S(1)} collective-permute-done((bf16[32,4096]{1,0:T(8,128)(2,1)S(1)}, bf16[32,4096]{1,0:T(8,128)(2,1)S(1)}, u32[]{:S(2)}, u32[]{:S(2)}) %collective-permute-start.2) | collective-permute-done | bytes 262176 | tf_op jit(solution)/shard_map/ppermute | solution.py:13
  296.1 35.0 %reduce-scatter.11.cloned.1.call-done = bf16[256,1024]{1,0:T(8,128)(2,1)} async-done(((bf16[1024,1024]{1,0:T(8,128)(2,1)}), bf16[256,1024]{1,0:T(8,128)(2,1)}) %reduce-scatter.11.cloned.1.call-update) | async-done | bytes 524304 | tf_op jit(solution)/shard_map/reduce_scatter | solution.py:94
  331.2 2.1 bitcast_convert_fusion
  333.3 0.7 copy.74
  (54 shorter events, 0.7 us)
Async XLA Ops:
  7.2 16.2 %copy-start = (bf16[1,256,4096]{2,1,0:T(8,128)(2,1)S(1)}, bf16[1,256,4096]{2,1,0:T(8,128)(2,1)}, u32[]{:S(2)}) copy-start(bf16[1,256,4096]{2,1,0:T(8,128)(2,1)} %param.13) | copy-start | bytes 6291460
  7.2 47.8 %reduce-scatter.5.cloned.1.call-start = ((), (), s32[]{:S(2)}) async-start(), calls=%async_computation.4 | async-start | bytes 1310720 | tf_op jit(solution)/shard_map/reduce_scatter | solution.py:72
  8.2 8.9 %copy-start.2 = (bf16[1,1,128,4096]{3,2,1,0:T(8,128)(2,1)S(1)}, bf16[1,1,128,4096]{3,2,1,0:T(8,128)(2,1)}, u32[]{:S(2)}) copy-start(bf16[1,1,128,4096]{3,2,1,0:T(8,128)(2,1)} %param.9) | copy-start | bytes 3145732
  17.1 0.7 copy-start.11
  24.9 68.6 %all-gather.5.cloned.1.call-start = ((), (), s32[]{:S(2)}) async-start(), calls=%async_computation.5 | async-start | bytes 1310720 | tf_op jit(solution)/shard_map/all_gather | solution.py:69
  56.1 8.5 %collective-permute-start = (bf16[32,4096]{1,0:T(8,128)(2,1)S(1)}, bf16[32,4096]{1,0:T(8,128)(2,1)S(1)}, u32[]{:S(2)}, u32[]{:S(2)}) collective-permute-start(bf16[32,4096]{1,0:T(8,128)(2,1)S(1)} %get-tuple-element.3), channel_id=1, source_target_pairs={{0,8},{8,16},{16,24},{1,9},{9,17},{17,25},{2,10},{10,18},{18,26},{... | collective-permute-start | bytes 786440 | tf_op jit(solution)/shard_map/ppermute | solution.py:13
  64.7 0.7 copy-start.7
  65.4 65.1 %reduce-scatter.7.cloned.1.call-start = ((), (), s32[]{:S(2)}) async-start(), calls=%async_computation.6 | async-start | bytes 1310720 | tf_op jit(solution)/shard_map/reduce_scatter | solution.py:72
  93.4 3.2 copy-start.3
  102.2 28.3 %copy-start.8 = (bf16[32,4096]{1,0:T(8,128)(2,1)S(1)}, bf16[32,4096]{1,0:T(8,128)(2,1)}, u32[]{:S(2)}) copy-start(bf16[32,4096]{1,0:T(8,128)(2,1)} %copy-done.7) | copy-start | bytes 786436
  103.7 65.2 %all-gather.7.cloned.1.call-start = ((), (), s32[]{:S(2)}) async-start(), calls=%async_computation.7 | async-start | bytes 1310720 | tf_op jit(solution)/shard_map/all_gather | solution.py:69
  131.7 8.5 %collective-permute-start.1 = (bf16[32,4096]{1,0:T(8,128)(2,1)S(1)}, bf16[32,4096]{1,0:T(8,128)(2,1)S(1)}, u32[]{:S(2)}, u32[]{:S(2)}) collective-permute-start(bf16[32,4096]{1,0:T(8,128)(2,1)S(1)} %get-tuple-element.5), channel_id=1, source_target_pairs={{0,8},{8,16},{16,24},{1,9},{9,17},{17,25},{2,10},{10,18},{18,26},{... | collective-permute-start | bytes 786440 | tf_op jit(solution)/shard_map/ppermute | solution.py:13
  140.2 0.7 copy-start.5
  140.9 65.1 %reduce-scatter.9.cloned.1.call-start = ((), (), s32[]{:S(2)}) async-start(), calls=%async_computation.8 | async-start | bytes 1310720 | tf_op jit(solution)/shard_map/reduce_scatter | solution.py:72
  168.9 3.2 copy-start.4
  177.7 28.3 %copy-start.6 = (bf16[32,4096]{1,0:T(8,128)(2,1)S(1)}, bf16[32,4096]{1,0:T(8,128)(2,1)}, u32[]{:S(2)}) copy-start(bf16[32,4096]{1,0:T(8,128)(2,1)} %copy-done.5) | copy-start | bytes 786436
  179.2 28.3 %copy-start.9 = (f32[4096]{0:T(1024)S(1)}, f32[4096]{0:T(1024)}, u32[]{:S(2)}) copy-start(f32[4096]{0:T(1024)} %param.14) | copy-start | bytes 49156
  179.2 38.0 %all-gather.9.cloned.1.call-start = ((), (), s32[]{:S(2)}) async-start(), calls=%async_computation.11 | async-start | bytes 2359296 | tf_op jit(solution)/shard_map/all_gather | solution.py:82
  208.8 73.5 %all-reduce.2.cloned.1.call-start = ((), (), s32[]{:S(2)}) async-start(), calls=%async_computation.9 | async-start | bytes 3145728 | tf_op jit(solution)/shard_map/psum | solution.py:18
  208.8 9.7 %copy-start.1 = (bf16[1,3,2,32,1024]{4,3,2,1,0:T(8,128)(2,1)S(1)}, bf16[1,3,2,32,1024]{4,3,2,1,0:T(8,128)(2,1)}, u32[]{:S(2)}) copy-start(bf16[1,3,2,32,1024]{4,3,2,1,0:T(8,128)(2,1)} %param.15) | copy-start | bytes 1179652
  208.8 10.3 %copy-start.10 = (f32[1,1024]{1,0:T(1,128)S(1)}, f32[1,1024]{1,0:T(1,128)}, u32[]{:S(2)}) copy-start(f32[1,1024]{1,0:T(1,128)} %param.16) | copy-start | bytes 12292
  218.5 112.7 %reduce-scatter.11.cloned.1.call-start = ((), (), s32[]{:S(2)}) async-start(), calls=%async_computation.10 | async-start | bytes 2621440 | tf_op jit(solution)/shard_map/reduce_scatter | solution.py:94
  287.4 8.8 %collective-permute-start.2 = (bf16[32,4096]{1,0:T(8,128)(2,1)S(1)}, bf16[32,4096]{1,0:T(8,128)(2,1)S(1)}, u32[]{:S(2)}, u32[]{:S(2)}) collective-permute-start(bf16[32,4096]{1,0:T(8,128)(2,1)S(1)} %get-tuple-element.7), channel_id=1, source_target_pairs={{0,8},{8,16},{16,24},{1,9},{9,17},{17,25},{2,10},{10,18},{18,26},{... | collective-permute-start | bytes 786440 | tf_op jit(solution)/shard_map/ppermute | solution.py:13
Sparse Core Ops, SparseCore 0:
  25.0 29.9 reduce-scatter.4
  65.5 27.8 all-gather.4
  103.8 26.6 reduce-scatter.6
  141.1 27.8 all-gather.6
  179.3 26.6 reduce-scatter.8
  208.9 8.2 all-gather.8
  220.3 61.9 all-reduce.1
  287.5 43.6 reduce-scatter.10
where the time goes:
time: 342 us; the launch traced here: 341 us
  waiting for transfers between devices  261 us (76%)
  matrix products  24.5 us (7%)
  other arithmetic  17.2 us (5%)
  between operations  14.5 us (4%)
  local copies, waits for them, and re-layouts  13.5 us (4%)
  starting transfers between devices  10.5 us (3%)
    reduce_scatter x3, waiting for transfers between devices, on_device(): lax.psum_scatter(partial_value.astype(jnp.bfloat16), 'dp', scatter_dimens...  83.1 us
    psum x1, waiting for transfers between devices, broadcast(): return lax.psum(kept, axis)  62.6 us
    all_gather x2, waiting for transfers between devices, on_device(): whole = lax.all_gather(own_rows, 'dp', axis=0, tiled=True)  55.8 us
    reduce_scatter x1, waiting for transfers between devices, on_device(): lax.psum_scatter(term.astype(jnp.bfloat16), 'dp', scatter_dimension=0, ti...  35 us
    ppermute x3, waiting for transfers between devices, shifted(): return lax.ppermute(x, axis, pairs)  15.6 us
    dot_general x3, matrix products, attend(): jnp.dot(normed, weights_qkv, preferred_element_type=jnp.float32)  15.1 us
    unnamed x29, local copies, waits for them, and re-layouts  11.1 us
    ppermute x3, starting transfers between devices, shifted(): return lax.ppermute(x, axis, pairs)  10.2 us
  transfers between devices with their start and end apart: 11, of which 11 were waited for; matrix products, arithmetic and copies ran while one was open for 0% of the time, Pallas kernels for 0%

commit v1 on v0

--- a/solution.py
+++ b/solution.py
@@ -1,3 +1,4 @@
+import functools
 import jax
 import jax.numpy as jnp
 from jax import lax
@@ -5,6 +6,35 @@
 
 HEAD_SIZE = 128
 TOK = 128
+
+
+def stages_all_map(local_block, d0):
+    s_next = list(local_block.shape[1:])
+    s_next[d0] *= local_block.shape[0]
+    return jnp.moveaxis(local_block, 0, d0).reshape(s_next)
+
+
+def keep_up_ranges_over_axis(s0, peer_axis, k_dim):
+    q_n = jax.lax.axis_size(peer_axis)
+    all_blocks = [(it, (it + 1) % q_n) for it in range(q_n)]
+    inbox = [(jj, dev_i) for dev_i, jj in all_blocks]
+    side_arr, a_now = ([], [])
+    for dev_j in tuple(range(q_n - 1)):
+        if dev_j % 2 == 0:
+            x_new = jax.lax.ppermute(side_arr[-1] if side_arr else s0, peer_axis, perm=all_blocks)
+            side_arr.append(x_new)
+        else:
+            reached = jax.lax.ppermute(a_now[-1] if a_now else s0, peer_axis, perm=inbox)
+            a_now.append(reached)
+    finding = jnp.stack([*side_arr[::-1], s0, *a_now])
+    found_now = jax.lax.axis_index(peer_axis)
+    big = len(side_arr)
+    current_value = found_now - big
+    finding = finding[(jnp.arange(q_n) - current_value) % q_n]
+    return stages_all_map(finding, k_dim)
+
+
+scales_resolve = functools.partial(keep_up_ranges_over_axis, peer_axis="dp", k_dim=0)
 
 
 def shifted(x, axis, by):
@@ -66,7 +96,7 @@
     own_rows = lax.dynamic_slice_in_dim(whole, first_row, share, 0)
     for tick in range(ticks):
         if tick > 0:
-            whole = lax.all_gather(own_rows, "dp", axis=0, tiled=True)
+            whole = scales_resolve(own_rows)
         crops = lax.dynamic_index_in_dim(crop_table, section - tick, 0, keepdims=False)
         partial_value = attend(whole, crops, gain, weights_qkv, weights_out)
         summed = lax.psum_scatter(

time: 342 us -> 326 us (0.953)
  waiting for transfers between devices: 261 us -> 235 us
  starting transfers between devices: 10.5 us -> 18.8 us
    all_gather x2 -> x0, waiting for transfers between devices: 55.8 us -> none  [on_device(): whole = lax.all_gather(own_rows, 'dp', axis=0, tiled=True)]
    ppermute x0 -> x6, waiting for transfers between devices: none -> 31.5 us  [the longest x4 27.6 us: keep_up_ranges_over_axis(): jax.lax.ppermute(side_arr[-1] if side_arr else s0, peer_axis, perm=all_bl...]
    ppermute x0 -> x6, starting transfers between devices: none -> 8.17 us  [the longest x2 7.69 us: keep_up_ranges_over_axis(): jax.lax.ppermute(a_now[-1] if a_now else s0, peer_axis, perm=inbox)]
    gather x0 -> x2, local copies, waits for them, and re-layouts: none -> 3.67 us  [keep_up_ranges_over_axis(): finding = finding[(jnp.arange(q_n) - current_value) % q_n]]
  transfers between devices with their start and end apart: 11 -> 15, of which waited for: 11 -> 15; matrix products, arithmetic and copies ran while one was open for 0% -> 1% of each run, Pallas kernels for 0% -> 0%
where the time goes in v1:
time: 326 us; the launch traced here: 325 us
  waiting for transfers between devices  235 us (72%)
  matrix products  24.5 us (8%)
  starting transfers between devices  18.8 us (6%)
  local copies, waits for them, and re-layouts  16.5 us (5%)
  other arithmetic  15.2 us (5%)
  between operations  14.5 us (4%)
    reduce_scatter x3, waiting for transfers between devices, on_device(): lax.psum_scatter(partial_value.astype(jnp.bfloat16), 'dp', scatter_dimens...  82.4 us
    psum x1, waiting for transfers between devices, broadcast(): return lax.psum(kept, axis)  62.4 us
    reduce_scatter x1, waiting for transfers between devices, on_device(): lax.psum_scatter(term.astype(jnp.bfloat16), 'dp', scatter_dimension=0, ti...  35 us
    ppermute x4, waiting for transfers between devices, keep_up_ranges_over_axis(): jax.lax.ppermute(side_arr[-1] if side_arr else s0, peer_axis, perm=all_bl...  27.6 us
    ppermute x3, waiting for transfers between devices, shifted(): return lax.ppermute(x, axis, pairs)  15.7 us
    dot_general x3, matrix products, attend(): jnp.dot(normed, weights_qkv, preferred_element_type=jnp.float32)  15 us
    unnamed x29, local copies, waits for them, and re-layouts  10.4 us
    ppermute x3, starting transfers between devices, shifted(): return lax.ppermute(x, axis, pairs)  10.2 us
  transfers between devices with their start and end apart: 15, of which 15 were waited for; matrix products, arithmetic and copies ran while one was open for 1% of the time, Pallas kernels for 0%

profile of v1, /device:TPU:0, one launch (start us, length us, event | category | flops | bytes accessed | tf_op | source)
XLA Modules:
  0.0 324.9 jit_solution(3429477982972746129)
XLA Ops:
  7.2 0.8 fusion.95
  8.2 8.9 %copy.23 = bf16[1,4096,3,256]{1,3,2,0:T(8,128)(2,1)} copy(bf16[1,4096,3,256]{3,1,2,0:T(8,128)(2,1)} %param.12) | data formatting | bytes 12582912 | tf_op args[3]
  17.1 0.2 convert_reduce_fusion
  17.3 0.4 fusion.18
  17.8 5.0 %convolution_convert_fusion.6 = bf16[128,768]{1,0:T(8,128)(2,1)S(1)} fusion(bf16[4096,768]{0,1:T(8,128)(2,1)} %bitcast.143, bf16[1,1,128,4096]{3,2,1,0:T(8,128)(2,1)S(1)} %copy-done.2, f32[4096]{0:T(1024)S(1)} %bitcast.160, f32[128]{0:T(128)S(1)} %add_rsqrt_fusion.6, f32[128]{0:T(128)S(1)} %broadcast_multiply_fusion.6), kind=kOutput, calls=%fused_computation.43 | convolution fusion | flops 808026112 | bytes 7554048 | tf_op jit(solution)/shard_map/dot_general | solution.py:63
  22.8 0.2 fusion.41
  23.2 0.2 convolution_convert_fusion.9
  23.4 1.4 convolution_convert_fusion.2
  24.9 30.1 %reduce-scatter.5.cloned.1.call-done = bf16[32,4096]{1,0:T(8,128)(2,1)} async-done(((bf16[128,4096]{1,0:T(8,128)(2,1)}), bf16[32,4096]{1,0:T(8,128)(2,1)}) %reduce-scatter.5.cloned.1.call-update) | async-done | bytes 262160 | tf_op jit(solution)/shard_map/reduce_scatter | solution.py:102
  55.0 1.1 convert_reduce_fusion.5
  56.1 3.4 %collective-permute-start = (bf16[32,4096]{1,0:T(8,128)(2,1)S(1)}, bf16[32,4096]{1,0:T(8,128)(2,1)S(1)}, u32[]{:S(2)}, u32[]{:S(2)}) collective-permute-start(bf16[32,4096]{1,0:T(8,128)(2,1)S(1)} %get-tuple-element.3), channel_id=1, source_target_pairs={{0,8},{8,16},{16,24},{1,9},{9,17},{17,25},{2,10},{10,18},{18,26},{... | collective-permute-start | bytes 786440 | tf_op jit(solution)/shard_map/ppermute | solution.py:43
  59.5 5.1 %collective-permute-done = bf16[32,4096]{1,0:T(8,128)(2,1)S(1)} collective-permute-done((bf16[32,4096]{1,0:T(8,128)(2,1)S(1)}, bf16[32,4096]{1,0:T(8,128)(2,1)S(1)}, u32[]{:S(2)}, u32[]{:S(2)}) %collective-permute-start) | collective-permute-done | bytes 262176 | tf_op jit(solution)/shard_map/ppermute | solution.py:43
  64.7 3.9 %collective-permute-start.3 = (bf16[32,4096]{1,0:T(8,128)(2,1)S(1)}, bf16[32,4096]{1,0:T(8,128)(2,1)S(1)}, u32[]{:S(2)}, u32[]{:S(2)}) collective-permute-start(bf16[32,4096]{1,0:T(8,128)(2,1)S(1)} %collective-permute-done), channel_id=1, source_target_pairs={{1,0},{2,1},{3,2},{0,3},{5,4},{6,5},{7,6},{4,7},{9,8},{10,9},{11,1... | collective-permute-start | bytes 786440 | tf_op jit(solution)/shard_map/ppermute | solution.py:27
  68.6 7.1 %collective-permute-done.1 = bf16[32,4096]{1,0:T(8,128)(2,1)S(1)} collective-permute-done((bf16[32,4096]{1,0:T(8,128)(2,1)S(1)}, bf16[32,4096]{1,0:T(8,128)(2,1)S(1)}, u32[]{:S(2)}, u32[]{:S(2)}) %collective-permute-start.1) | collective-permute-done | bytes 262176 | tf_op jit(solution)/shard_map/ppermute | solution.py:24
  75.7 0.2 collective-permute-start.2
  76.0 2.0 collective-permute-done.3
  78.0 6.6 %collective-permute-done.2 = bf16[32,4096]{1,0:T(8,128)(2,1)S(1)} collective-permute-done((bf16[32,4096]{1,0:T(8,128)(2,1)S(1)}, bf16[32,4096]{1,0:T(8,128)(2,1)S(1)}, u32[]{:S(2)}, u32[]{:S(2)}) %collective-permute-start.2) | collective-permute-done | bytes 262176 | tf_op jit(solution)/shard_map/ppermute | solution.py:24
  84.6 1.1 pad_maximum_fusion
  85.7 1.8 gather_fusion
  87.5 0.2 convert_reduce_fusion.2
  87.8 0.4 fusion.10
  88.2 0.4 fusion.12
  88.6 5.0 %convolution_convert_fusion.5 = bf16[128,768]{1,0:T(8,128)(2,1)S(1)} fusion(bf16[128,4096]{1,0:T(8,128)(2,1)S(1)} %bitcast.148, bf16[4096,768]{0,1:T(8,128)(2,1)} %bitcast.144), kind=kOutput, calls=%fused_computation.42 | convolution fusion | flops 805404672 | bytes 7536640 | tf_op jit(solution)/shard_map/dot_general | solution.py:63
  94.0 0.2 convolution_convert_fusion.8
  94.2 1.4 convolution_convert_fusion.1
  95.7 26.5 %reduce-scatter.7.cloned.1.call-done = bf16[32,4096]{1,0:T(8,128)(2,1)} async-done(((bf16[128,4096]{1,0:T(8,128)(2,1)}), bf16[32,4096]{1,0:T(8,128)(2,1)}) %reduce-scatter.7.cloned.1.call-update) | async-done | bytes 262160 | tf_op jit(solution)/shard_map/reduce_scatter | solution.py:102
  122.2 1.1 convert_reduce_fusion.4
  123.4 0.7 copy-done.3
  124.1 3.4 %collective-permute-start.4 = (bf16[32,4096]{1,0:T(8,128)(2,1)S(1)}, bf16[32,4096]{1,0:T(8,128)(2,1)S(1)}, u32[]{:S(2)}, u32[]{:S(2)}) collective-permute-start(bf16[32,4096]{1,0:T(8,128)(2,1)S(1)} %get-tuple-element.5), channel_id=1, source_target_pairs={{0,8},{8,16},{16,24},{1,9},{9,17},{17,25},{2,10},{10,18},{18,26},{... | collective-permute-start | bytes 786440 | tf_op jit(solution)/shard_map/ppermute | solution.py:43
  127.5 5.1 %collective-permute-done.4 = bf16[32,4096]{1,0:T(8,128)(2,1)S(1)} collective-permute-done((bf16[32,4096]{1,0:T(8,128)(2,1)S(1)}, bf16[32,4096]{1,0:T(8,128)(2,1)S(1)}, u32[]{:S(2)}, u32[]{:S(2)}) %collective-permute-start.4) | collective-permute-done | bytes 262176 | tf_op jit(solution)/shard_map/ppermute | solution.py:43
  132.6 3.8 %collective-permute-start.7 = (bf16[32,4096]{1,0:T(8,128)(2,1)S(1)}, bf16[32,4096]{1,0:T(8,128)(2,1)S(1)}, u32[]{:S(2)}, u32[]{:S(2)}) collective-permute-start(bf16[32,4096]{1,0:T(8,128)(2,1)S(1)} %collective-permute-done.4), channel_id=1, source_target_pairs={{1,0},{2,1},{3,2},{0,3},{5,4},{6,5},{7,6},{4,7},{9,8},{10,9},{11,1... | collective-permute-start | bytes 786440 | tf_op jit(solution)/shard_map/ppermute | solution.py:27
  136.5 7.2 %collective-permute-done.5 = bf16[32,4096]{1,0:T(8,128)(2,1)S(1)} collective-permute-done((bf16[32,4096]{1,0:T(8,128)(2,1)S(1)}, bf16[32,4096]{1,0:T(8,128)(2,1)S(1)}, u32[]{:S(2)}, u32[]{:S(2)}) %collective-permute-start.5) | collective-permute-done | bytes 262176 | tf_op jit(solution)/shard_map/ppermute | solution.py:24
  143.6 0.2 collective-permute-start.6
  143.8 1.9 collective-permute-done.7
  145.7 6.8 %collective-permute-done.6 = bf16[32,4096]{1,0:T(8,128)(2,1)S(1)} collective-permute-done((bf16[32,4096]{1,0:T(8,128)(2,1)S(1)}, bf16[32,4096]{1,0:T(8,128)(2,1)S(1)}, u32[]{:S(2)}, u32[]{:S(2)}) %collective-permute-start.6) | collective-permute-done | bytes 262176 | tf_op jit(solution)/shard_map/ppermute | solution.py:24
  152.5 1.1 pad_maximum_fusion.1
  153.6 1.8 gather_fusion.1
  155.5 0.2 convert_reduce_fusion.1
  155.7 0.4 fusion.7
  156.1 0.4 fusion.9
  156.6 5.0 %convolution_convert_fusion.4 = bf16[128,768]{1,0:T(8,128)(2,1)S(1)} fusion(bf16[128,4096]{1,0:T(8,128)(2,1)S(1)} %bitcast.147, bf16[4096,768]{0,1:T(8,128)(2,1)} %bitcast.145), kind=kOutput, calls=%fused_computation.41 | convolution fusion | flops 805404672 | bytes 7536640 | tf_op jit(solution)/shard_map/dot_general | solution.py:63
  161.9 0.2 convolution_convert_fusion.7
  162.2 1.4 convolution_convert_fusion
  163.6 0.2 all-gather.3.cloned.1.call-start
  163.9 0.3 fusion.67
  164.1 0.3 fusion.64
  164.4 25.8 %reduce-scatter.9.cloned.1.call-done = bf16[32,4096]{1,0:T(8,128)(2,1)} async-done(((bf16[128,4096]{1,0:T(8,128)(2,1)}), bf16[32,4096]{1,0:T(8,128)(2,1)}) %reduce-scatter.9.cloned.1.call-update) | async-done | bytes 262160 | tf_op jit(solution)/shard_map/reduce_scatter | solution.py:102
  190.2 1.1 convert_reduce_fusion.3
  191.3 0.3 fusion.61
  191.6 0.3 fusion.72
  191.9 1.0 pad_maximum_fusion.2
  193.0 8.4 %all-gather.3.cloned.1.call-done = bf16[3,64,4096]{2,1,0:T(8,128)(2,1)} async-done(((bf16[3,32,4096]{2,1,0:T(8,128)(2,1)}), bf16[3,64,4096]{2,1,0:T(8,128)(2,1)}) %all-gather.3.cloned.1.call-update) | async-done | bytes 1572880 | tf_op jit(solution)/shard_map/all_gather | solution.py:112
  201.4 1.3 broadcast_select_fusion
  203.0 0.2 fusion.51
  203.3 0.3 fusion.54
  203.6 0.2 multiply_convert_fusion
  203.8 62.4 %all-reduce.2.cloned.1.call-done = bf16[3,2,32,4096]{3,2,1,0:T(8,128)(2,1)} async-done(((bf16[3,2,32,4096]{3,2,1,0:T(8,128)(2,1)}), bf16[3,2,32,4096]{3,2,1,0:T(8,128)(2,1)}) %all-reduce.2.cloned.1.call-update) | async-done | bytes 1572880 | tf_op jit(solution)/shard_map/psum | solution.py:48
  266.3 1.0 constant_dynamic-slice_fusion
  267.3 4.1 %convolution_convert_fusion.3 = bf16[1024,1024]{1,0:T(8,128)(2,1)} fusion(bf16[192,1024]{1,0:T(8,128)(2,1)S(1)} %fusion.54, bf16[192,1024]{1,0:T(8,128)(2,1)S(1)} %bitcast.149, bf16[1,1024,1024]{2,1,0:T(8,128)(2,1)} %param.17, bf16[192,1024]{1,0:T(8,128)(2,1)S(1)} %bitcast.150), kind=kOutput, calls=%fused_computation.36 | convolution fusion | flops 807141376 | bytes 5373952 | tf_op jit(solution)/shard_map/dot_general | solution.py:123
  271.4 3.4 %collective-permute-start.8 = (bf16[32,4096]{1,0:T(8,128)(2,1)S(1)}, bf16[32,4096]{1,0:T(8,128)(2,1)S(1)}, u32[]{:S(2)}, u32[]{:S(2)}) collective-permute-start(bf16[32,4096]{1,0:T(8,128)(2,1)S(1)} %get-tuple-element.7), channel_id=1, source_target_pairs={{0,8},{8,16},{16,24},{1,9},{9,17},{17,25},{2,10},{10,18},{18,26},{... | collective-permute-start | bytes 786440 | tf_op jit(solution)/shard_map/ppermute | solution.py:43
  274.8 5.4 %collective-permute-done.8 = bf16[32,4096]{1,0:T(8,128)(2,1)S(1)} collective-permute-done((bf16[32,4096]{1,0:T(8,128)(2,1)S(1)}, bf16[32,4096]{1,0:T(8,128)(2,1)S(1)}, u32[]{:S(2)}, u32[]{:S(2)}) %collective-permute-start.8) | collective-permute-done | bytes 262176 | tf_op jit(solution)/shard_map/ppermute | solution.py:43
  280.2 35.0 %reduce-scatter.11.cloned.1.call-done = bf16[256,1024]{1,0:T(8,128)(2,1)} async-done(((bf16[1024,1024]{1,0:T(8,128)(2,1)}), bf16[256,1024]{1,0:T(8,128)(2,1)}) %reduce-scatter.11.cloned.1.call-update) | async-done | bytes 524304 | tf_op jit(solution)/shard_map/reduce_scatter | solution.py:124
  315.2 2.1 bitcast_convert_fusion
  317.3 0.7 copy.74
  (68 shorter events, 1.9 us)
Async XLA Ops:
  7.2 16.2 %copy-start = (bf16[1,256,4096]{2,1,0:T(8,128)(2,1)S(1)}, bf16[1,256,4096]{2,1,0:T(8,128)(2,1)}, u32[]{:S(2)}) copy-start(bf16[1,256,4096]{2,1,0:T(8,128)(2,1)} %param.13) | copy-start | bytes 6291460
  7.2 47.8 %reduce-scatter.5.cloned.1.call-start = ((), (), s32[]{:S(2)}) async-start(), calls=%async_computation.4 | async-start | bytes 1310720 | tf_op jit(solution)/shard_map/reduce_scatter | solution.py:102
  8.2 8.9 %copy-start.2 = (bf16[1,1,128,4096]{3,2,1,0:T(8,128)(2,1)S(1)}, bf16[1,1,128,4096]{3,2,1,0:T(8,128)(2,1)}, u32[]{:S(2)}) copy-start(bf16[1,1,128,4096]{3,2,1,0:T(8,128)(2,1)} %param.9) | copy-start | bytes 3145732
  17.1 0.7 copy-start.9
  24.8 97.4 %reduce-scatter.7.cloned.1.call-start = ((), (), s32[]{:S(2)}) async-start(), calls=%async_computation.5 | async-start | bytes 1310720 | tf_op jit(solution)/shard_map/reduce_scatter | solution.py:102
  56.1 8.5 %collective-permute-start = (bf16[32,4096]{1,0:T(8,128)(2,1)S(1)}, bf16[32,4096]{1,0:T(8,128)(2,1)S(1)}, u32[]{:S(2)}, u32[]{:S(2)}) collective-permute-start(bf16[32,4096]{1,0:T(8,128)(2,1)S(1)} %get-tuple-element.3), channel_id=1, source_target_pairs={{0,8},{8,16},{16,24},{1,9},{9,17},{17,25},{2,10},{10,18},{18,26},{... | collective-permute-start | bytes 786440 | tf_op jit(solution)/shard_map/ppermute | solution.py:43
  64.7 19.9 %copy-start.7 = (bf16[32,4096]{1,0:T(8,128)(2,1)}, bf16[32,4096]{1,0:T(8,128)(2,1)S(1)}, u32[]{:S(2)}) copy-start(bf16[32,4096]{1,0:T(8,128)(2,1)S(1)} %collective-permute-done) | copy-start | bytes 786436
  64.7 11.0 %collective-permute-start.1 = (bf16[32,4096]{1,0:T(8,128)(2,1)S(1)}, bf16[32,4096]{1,0:T(8,128)(2,1)S(1)}, u32[]{:S(2)}, u32[]{:S(2)}) collective-permute-start(bf16[32,4096]{1,0:T(8,128)(2,1)S(1)} %collective-permute-done), channel_id=1, source_target_pairs={{0,1},{1,2},{2,3},{3,0},{4,5},{5,6},{6,7},{7,4},{8,9},{9,10},{10,1... | collective-permute-start | bytes 786440 | tf_op jit(solution)/shard_map/ppermute | solution.py:24
  64.7 13.3 %collective-permute-start.3 = (bf16[32,4096]{1,0:T(8,128)(2,1)S(1)}, bf16[32,4096]{1,0:T(8,128)(2,1)S(1)}, u32[]{:S(2)}, u32[]{:S(2)}) collective-permute-start(bf16[32,4096]{1,0:T(8,128)(2,1)S(1)} %collective-permute-done), channel_id=1, source_target_pairs={{1,0},{2,1},{3,2},{0,3},{5,4},{6,5},{7,6},{4,7},{9,8},{10,9},{11,1... | collective-permute-start | bytes 786440 | tf_op jit(solution)/shard_map/ppermute | solution.py:27
  75.7 8.9 %collective-permute-start.2 = (bf16[32,4096]{1,0:T(8,128)(2,1)S(1)}, bf16[32,4096]{1,0:T(8,128)(2,1)S(1)}, u32[]{:S(2)}, u32[]{:S(2)}) collective-permute-start(bf16[32,4096]{1,0:T(8,128)(2,1)S(1)} %collective-permute-done.1), channel_id=1, source_target_pairs={{0,1},{1,2},{2,3},{3,0},{4,5},{5,6},{6,7},{7,4},{8,9},{9,10},{10,1... | collective-permute-start | bytes 786440 | tf_op jit(solution)/shard_map/ppermute | solution.py:24
  94.2 28.1 %copy-start.8 = (bf16[32,4096]{1,0:T(8,128)(2,1)S(1)}, bf16[32,4096]{1,0:T(8,128)(2,1)}, u32[]{:S(2)}) copy-start(bf16[32,4096]{1,0:T(8,128)(2,1)} %copy-done.7) | copy-start | bytes 786436
  95.7 94.5 %reduce-scatter.9.cloned.1.call-start = ((), (), s32[]{:S(2)}) async-start(), calls=%async_computation.6 | async-start | bytes 1310720 | tf_op jit(solution)/shard_map/reduce_scatter | solution.py:102
  123.4 0.7 copy-start.3
  124.1 8.5 %collective-permute-start.4 = (bf16[32,4096]{1,0:T(8,128)(2,1)S(1)}, bf16[32,4096]{1,0:T(8,128)(2,1)S(1)}, u32[]{:S(2)}, u32[]{:S(2)}) collective-permute-start(bf16[32,4096]{1,0:T(8,128)(2,1)S(1)} %get-tuple-element.5), channel_id=1, source_target_pairs={{0,8},{8,16},{16,24},{1,9},{9,17},{17,25},{2,10},{10,18},{18,26},{... | collective-permute-start | bytes 786440 | tf_op jit(solution)/shard_map/ppermute | solution.py:43
  132.6 19.9 %copy-start.5 = (bf16[32,4096]{1,0:T(8,128)(2,1)}, bf16[32,4096]{1,0:T(8,128)(2,1)S(1)}, u32[]{:S(2)}) copy-start(bf16[32,4096]{1,0:T(8,128)(2,1)S(1)} %collective-permute-done.4) | copy-start | bytes 786436
  132.6 11.0 %collective-permute-start.5 = (bf16[32,4096]{1,0:T(8,128)(2,1)S(1)}, bf16[32,4096]{1,0:T(8,128)(2,1)S(1)}, u32[]{:S(2)}, u32[]{:S(2)}) collective-permute-start(bf16[32,4096]{1,0:T(8,128)(2,1)S(1)} %collective-permute-done.4), channel_id=1, source_target_pairs={{0,1},{1,2},{2,3},{3,0},{4,5},{5,6},{6,7},{7,4},{8,9},{9,10},{10,1... | collective-permute-start | bytes 786440 | tf_op jit(solution)/shard_map/ppermute | solution.py:24
  132.6 13.1 %collective-permute-start.7 = (bf16[32,4096]{1,0:T(8,128)(2,1)S(1)}, bf16[32,4096]{1,0:T(8,128)(2,1)S(1)}, u32[]{:S(2)}, u32[]{:S(2)}) collective-permute-start(bf16[32,4096]{1,0:T(8,128)(2,1)S(1)} %collective-permute-done.4), channel_id=1, source_target_pairs={{1,0},{2,1},{3,2},{0,3},{5,4},{6,5},{7,6},{4,7},{9,8},{10,9},{11,1... | collective-permute-start | bytes 786440 | tf_op jit(solution)/shard_map/ppermute | solution.py:27
  143.6 8.9 %collective-permute-start.6 = (bf16[32,4096]{1,0:T(8,128)(2,1)S(1)}, bf16[32,4096]{1,0:T(8,128)(2,1)S(1)}, u32[]{:S(2)}, u32[]{:S(2)}) collective-permute-start(bf16[32,4096]{1,0:T(8,128)(2,1)S(1)} %collective-permute-done.5), channel_id=1, source_target_pairs={{0,1},{1,2},{2,3},{3,0},{4,5},{5,6},{6,7},{7,4},{8,9},{9,10},{10,1... | collective-permute-start | bytes 786440 | tf_op jit(solution)/shard_map/ppermute | solution.py:24
  162.1 2.0 copy-start.4
  162.1 28.1 %copy-start.6 = (bf16[32,4096]{1,0:T(8,128)(2,1)S(1)}, bf16[32,4096]{1,0:T(8,128)(2,1)}, u32[]{:S(2)}) copy-start(bf16[32,4096]{1,0:T(8,128)(2,1)} %copy-done.5) | copy-start | bytes 786436
  163.6 28.0 %copy-start.10 = (f32[4096]{0:T(1024)S(1)}, f32[4096]{0:T(1024)}, u32[]{:S(2)}) copy-start(f32[4096]{0:T(1024)} %param.14) | copy-start | bytes 49156
  163.6 37.8 %all-gather.3.cloned.1.call-start = ((), (), s32[]{:S(2)}) async-start(), calls=%async_computation.9 | async-start | bytes 2359296 | tf_op jit(solution)/shard_map/all_gather | solution.py:112
  192.9 73.4 %all-reduce.2.cloned.1.call-start = ((), (), s32[]{:S(2)}) async-start(), calls=%async_computation.7 | async-start | bytes 3145728 | tf_op jit(solution)/shard_map/psum | solution.py:48
  193.0 9.7 %copy-start.1 = (bf16[1,3,2,32,1024]{4,3,2,1,0:T(8,128)(2,1)S(1)}, bf16[1,3,2,32,1024]{4,3,2,1,0:T(8,128)(2,1)}, u32[]{:S(2)}) copy-start(bf16[1,3,2,32,1024]{4,3,2,1,0:T(8,128)(2,1)} %param.15) | copy-start | bytes 1179652
  193.0 10.3 %copy-start.11 = (f32[1,1024]{1,0:T(1,128)S(1)}, f32[1,1024]{1,0:T(1,128)}, u32[]{:S(2)}) copy-start(f32[1,1024]{1,0:T(1,128)} %param.16) | copy-start | bytes 12292
  202.7 112.5 %reduce-scatter.11.cloned.1.call-start = ((), (), s32[]{:S(2)}) async-start(), calls=%async_computation.8 | async-start | bytes 2621440 | tf_op jit(solution)/shard_map/reduce_scatter | solution.py:124
  271.4 8.8 %collective-permute-start.8 = (bf16[32,4096]{1,0:T(8,128)(2,1)S(1)}, bf16[32,4096]{1,0:T(8,128)(2,1)S(1)}, u32[]{:S(2)}, u32[]{:S(2)}) collective-permute-start(bf16[32,4096]{1,0:T(8,128)(2,1)S(1)} %get-tuple-element.7), channel_id=1, source_target_pairs={{0,8},{8,16},{16,24},{1,9},{9,17},{17,25},{2,10},{10,18},{18,26},{... | collective-permute-start | bytes 786440 | tf_op jit(solution)/shard_map/ppermute | solution.py:43
Sparse Core Ops, SparseCore 0:
  25.0 29.9 reduce-scatter.4
  95.8 26.4 reduce-scatter.6
  163.7 26.4 reduce-scatter.8
  193.0 8.2 all-gather.2
  204.3 61.9 all-reduce.1
  271.5 43.6 reduce-scatter.10
